TPU v7x, 32 devices: a whole 2x2x4 slice. The times are simulated.
32 devices in a mesh: shot: 4 (over y, x), rcv: 8 (over z, core).
Axes of the slice: x: 2, y: 2, z: 4, core: 2. Of those that a mesh axis runs over, the one named last changes fastest.
Arguments:
- modeled: bfloat16 [2, 32, 4, 64, 512], P(None, 'shot', None, 'rcv'), may hold values from -9 to 9
- observed: bfloat16 [2, 4, 32, 64, 512], P(None, 'shot', 'rcv'), may hold values from -60 to 60
- mask: int32 [32, 4, 64], P('shot', None, 'rcv'), may hold values 0 or 1
- shot_order: int32 [32], replicated, may hold values from 0 to 31, as said below
- line_of_slot: int32 [4], replicated, may hold values from 0 to 3, as said below
- coupling: bfloat16 [2, 512, 512], replicated, may hold values from -0.25 to 0.25
- wavelet: float32 [2, 512], replicated, may hold values from -4 to 4
- damping: float32 [512], replicated, may hold values from 2048 to 32768
Outputs:
- new_wavelet: float32 [2, 512], replicated
- residual_out: bfloat16 [2, 32, 4, 64, 512], P(None, 'shot', None, 'rcv')
Inputs may be any that keep to these rules, and one draw needn't show every extreme that they name: Group g holds the shots shot_order[g * 8] to shot_order[(g + 1) * 8 - 1]; each shot number appears once. `line_of_slot`: each line appears in exactly one slot.
All inputs are finite; a program needn't handle non-finite values. No bound on the sum of `mask` on one device may be relied on, other than what follows from the above.
Results may differ from a plain program's by a relative error of at most 0.00045.
Values may be sent and summed in bfloat16 or wider, within the bound.
A program may use at most 64 MiB of HBM per device.

v0:
```python
import jax
import jax.numpy as jnp
from jax import lax
from jax.sharding import PartitionSpec as P


def weigh(trace, coupling):
    real_part = jnp.dot(trace[0], coupling[0], preferred_element_type=jnp.float32) - jnp.dot(
        trace[1], coupling[1], preferred_element_type=jnp.float32
    )
    imag_part = jnp.dot(trace[0], coupling[1], preferred_element_type=jnp.float32) + jnp.dot(
        trace[1], coupling[0], preferred_element_type=jnp.float32
    )
    return jnp.stack([real_part, imag_part])


def per_device(modeled, observed, mask, shot_order, line_of_slot, coupling, wavelet, damping):
    group_size = modeled.shape[1]
    line_count = modeled.shape[2]
    slot_count = lax.axis_size("shot")
    stored = observed[:, 0]
    spread = lax.all_to_all(stored, "rcv", split_axis=2, concat_axis=1, tiled=True)
    grouped = jnp.take(spread, shot_order, axis=1)
    grouped = grouped.reshape(2, slot_count, group_size, grouped.shape[2], grouped.shape[3])
    arrived = lax.all_to_all(grouped, "shot", split_axis=1, concat_axis=1, tiled=True)
    inverse = (
        jnp.zeros((line_count,), jnp.int32)
        .at[line_of_slot]
        .set(jnp.arange(line_count, dtype=jnp.int32))
    )
    by_line = jnp.transpose(jnp.take(arrived, inverse, axis=1), (0, 2, 1, 3, 4))
    wd = weigh(by_line, coupling)
    wg = weigh(modeled, coupling)
    live = mask.astype(jnp.float32)[..., None]
    res_re = live * (wd[0] - (wavelet[0] * wg[0] - wavelet[1] * wg[1]))
    res_im = live * (wd[1] - (wavelet[0] * wg[1] + wavelet[1] * wg[0]))
    num_re = jnp.sum(wg[0] * res_re + wg[1] * res_im, axis=(0, 1, 2))
    num_im = jnp.sum(wg[0] * res_im - wg[1] * res_re, axis=(0, 1, 2))
    den = jnp.sum(live * (wg[0] * wg[0] + wg[1] * wg[1]), axis=(0, 1, 2))
    numerator = jnp.stack([num_re, num_im])
    numerator, den = lax.psum((numerator, den), ("shot", "rcv"))
    new_wavelet = wavelet + numerator / (den + damping)[None, :]
    out_re = live * (wd[0] - (new_wavelet[0] * wg[0] - new_wavelet[1] * wg[1]))
    out_im = live * (wd[1] - (new_wavelet[0] * wg[1] + new_wavelet[1] * wg[0]))
    return (new_wavelet, jnp.stack([out_re, out_im]).astype(jnp.bfloat16))


def solution(mesh):
    placed = (
        P(None, "shot", None, "rcv", None),
        P(None, "shot", "rcv", None, None),
        P("shot", None, "rcv"),
        P(),
        P(),
        P(),
        P(),
        P(),
    )
    return jax.shard_map(
        per_device,
        mesh=mesh,
        in_specs=placed,
        out_specs=(P(), P(None, "shot", None, "rcv", None)),
        check_vma=False,
    )
```

profile of v0, /device:TPU:10, one launch (start us, length us, event | category | flops | bytes accessed | tf_op | source)
XLA Modules:
  0.0 82.5 jit_solution(1885239426793906169)
XLA Ops:
  0.6 0.0 copy-start
  0.6 2.3 %copy.30 = bf16[2,1,4,64,512]{4,2,0,3,1:T(4,128)(2,1)} copy(bf16[2,1,4,64,512]{4,3,2,1,0:T(8,128)(2,1)} %param.9) | data formatting | bytes 1048576 | tf_op args[1]
  3.0 5.5 %all-to-all-start = ((bf16[2,4,64,512]{3,1,0,2:T(4,128)(2,1)}), bf16[2,4,64,512]{3,1,0,2:T(4,128)(2,1)S(1)}, u32[]{:S(2)}, u32[]{:S(2)}) async-start(bf16[2,4,64,512]{3,1,0,2:T(4,128)(2,1)} %bitcast.71), calls=%async_computation | async-start | bytes 1048576 | tf_op jit(solution)/shard_map/all_to_all | solution.py:22
  8.4 0.0 copy-done.7
  8.4 0.0 copy-start.8
  8.5 0.6 copy-done.8
  9.1 0.1 broadcast_in_dim.31
  9.2 0.6 scatter_custom_fusion
  9.8 0.1 copy-done.3
  9.9 0.0 copy-done
  9.9 1.1 %fusion.2 = f32[8,4,8,512]{3,2,1,0:T(8,128)} fusion(bf16[2,512,512]{2,1,0:T(8,128)(2,1)S(1)} %copy-done, bf16[2,8,4,8,512]{4,3,2,1,0:T(8,128)(2,1)S(1)} %copy-done.1), kind=kOutput, calls=%fused_computation.10 | convolution fusion | flops 134217728 | bytes 1310720 | tf_op jit(solution)/shard_map/dot_general | solution.py:11
  11.0 0.3 fusion.10
  11.3 9.2 %all-to-all-done = bf16[2,4,64,512]{3,1,0,2:T(4,128)(2,1)S(1)} async-done(((bf16[2,4,64,512]{3,1,0,2:T(4,128)(2,1)}), bf16[2,4,64,512]{3,1,0,2:T(4,128)(2,1)S(1)}, u32[]{:S(2)}, u32[]{:S(2)}) %all-to-all-start) | async-done | bytes 524320 | tf_op jit(solution)/shard_map/all_to_all | solution.py:22
  20.5 0.2 copy.29
  20.7 0.6 gather_fusion
  21.3 0.9 %copy_select_fusion.1 = bf16[2,4,8,8,512]{4,3,2,0,1:T(8,128)(2,1)} fusion(bf16[2,4,8,8,512]{4,3,0,2,1:T(8,128)(2,1)S(1)} %bitcast.75, pred[4,8]{1,0:T(4,128)(4,1)S(1)} %broadcast_in_dim.31), kind=kLoop, calls=%fused_computation.22 | loop fusion | flops 262144 | bytes 1048608 | tf_op jit(solution)/shard_map/jit(_take)/select_n | solution.py:23
  22.3 4.4 %all-to-all-start.1 = ((bf16[2,4,8,8,512]{4,3,2,0,1:T(8,128)(2,1)}), bf16[2,4,8,8,512]{4,3,2,0,1:T(8,128)(2,1)S(1)}, u32[]{:S(2)}, u32[]{:S(2)}) async-start(bf16[2,4,8,8,512]{4,3,2,0,1:T(8,128)(2,1)} %copy_select_fusion.1), calls=%async_computation.1 | async-start | bytes 1048576 | tf_op jit(solution)/shard_map/all_to_all | solution.py:25
  26.7 0.3 convolution_subtract_fusion.1
  27.0 7.1 %all-to-all-done.1 = bf16[2,4,8,8,512]{4,3,2,0,1:T(8,128)(2,1)S(1)} async-done(((bf16[2,4,8,8,512]{4,3,2,0,1:T(8,128)(2,1)}), bf16[2,4,8,8,512]{4,3,2,0,1:T(8,128)(2,1)S(1)}, u32[]{:S(2)}, u32[]{:S(2)}) %all-to-all-start.1) | async-done | bytes 524320 | tf_op jit(solution)/shard_map/all_to_all | solution.py:25
  34.1 0.6 gather_fusion.1
  34.7 0.1 fusion.12
  34.8 0.3 fusion
  35.1 0.3 fusion.8
  35.4 0.3 convolution_add_fusion
  35.7 0.3 convolution_subtract_fusion
  36.0 0.7 copy-done.2
  36.8 1.4 %add_reduce_fusion = (f32[512]{0:T(512)S(1)}, f32[512]{0:T(512)S(1)}, f32[512]{0:T(512)S(1)}, f32[8,4,8,512]{3,2,1,0:T(8,128)}) fusion(f32[8,4,8,512]{3,2,1,0:T(8,128)S(1)} %convolution_add_fusion, f32[8,4,8,512]{3,2,1,0:T(8,128)S(1)} %convolution_subtract_fusion.1, f32[8,4,8,512]{3,2,1,0:T(8,128)S(1)} %convolution_subtract_fusion, f32[512]{0:T(512)S(1)} %bitcast.79, ...), kind=kOutput, calls=%fused_computation.29 | convolution fusion | flops 137361920 | bytes 3434496 | tf_op jit(solution)/shard_map/dot_general | solution.py:11
  38.2 41.5 %all-reduce = (f32[2,512]{1,0:T(2,128)S(1)}, f32[512]{0:T(512)S(1)}) all-reduce(f32[2,512]{1,0:T(2,128)S(1)} %pad_maximum_fusion.1, f32[512]{0:T(512)S(1)} %get-tuple-element.4), channel_id=1, replica_groups=mesh['shot'=4,'rcv'=8] {'shot','rcv'}, use_global_device_ids=true, to_apply=%region_3.4 | all-reduce | flops 1536 | bytes 12288 | tf_op jit(solution)/shard_map/psum | solution.py:41
  79.8 0.0 copy-start.4
  79.8 0.6 copy-done.4
  80.4 1.3 %fusion.21 = (bf16[1,8,4,8,512]{4,3,2,1,0:T(8,128)(2,1)S(1)}, bf16[1,8,4,8,512]{4,3,2,1,0:T(8,128)(2,1)S(1)}) fusion(f32[8,4,8,512]{3,2,1,0:T(8,128)S(1)} %convolution_subtract_fusion, f32[8,4,8,512]{3,2,1,0:T(8,128)} %get-tuple-element.13, f32[8,4,8,512]{3,2,1,0:T(8,128)S(1)} %convolution_subtract_fusion.1, f32[512]{0:T(512)S(1)} %bitcast.77, ...), kind=kLoop, calls=%fused_computation.40 | loop fusion | flops 1572864 | bytes 2626560 | tf_op jit(solution)/shard_map/stack | solution.py:45
  81.6 0.8 %pad_maximum_fusion = bf16[2,8,4,8,512]{4,3,2,1,0:T(8,128)(2,1)} fusion(bf16[1,8,4,8,512]{4,3,2,1,0:T(8,128)(2,1)S(1)} %get-tuple-element.8, bf16[1,8,4,8,512]{4,3,2,1,0:T(8,128)(2,1)S(1)} %get-tuple-element.7), kind=kLoop, calls=%fused_computation.7 | loop fusion | flops 262144 | bytes 1048576 | tf_op jit(solution)/shard_map/stack | solution.py:45
  (25 shorter events, 0.2 us)
Async XLA Ops:
  0.6 9.3 %copy-start = (bf16[2,512,512]{2,1,0:T(8,128)(2,1)S(1)}, bf16[2,512,512]{2,1,0:T(8,128)(2,1)}, u32[]{:S(2)}) copy-start(bf16[2,512,512]{2,1,0:T(8,128)(2,1)} %param.13) | copy-start | bytes 3145732
  3.0 5.5 %copy-start.7 = (s32[32]{0:T(128)S(1)}, s32[32]{0:T(128)}, u32[]{:S(2)}) copy-start(s32[32]{0:T(128)} %param.11) | copy-start | bytes 388
  3.0 6.9 %copy-start.1 = (bf16[2,8,4,8,512]{4,3,2,1,0:T(8,128)(2,1)S(1)}, bf16[2,8,4,8,512]{4,3,2,1,0:T(8,128)(2,1)}, u32[]{:S(2)}) copy-start(bf16[2,8,4,8,512]{4,3,2,1,0:T(8,128)(2,1)} %param.8) | copy-start | bytes 1572868
  3.0 17.6 %all-to-all-start = ((bf16[2,4,64,512]{3,1,0,2:T(4,128)(2,1)}), bf16[2,4,64,512]{3,1,0,2:T(4,128)(2,1)S(1)}, u32[]{:S(2)}, u32[]{:S(2)}) async-start(bf16[2,4,64,512]{3,1,0,2:T(4,128)(2,1)} %bitcast.71), calls=%async_computation | async-start | bytes 1048576 | tf_op jit(solution)/shard_map/all_to_all | solution.py:22
  8.4 0.7 copy-start.8
  9.2 0.7 copy-start.3
  22.2 4.4 %copy-start.5 = (s32[8,4,8]{2,1,0:T(4,128)S(1)}, s32[8,4,8]{2,1,0:T(4,128)}, u32[]{:S(2)}) copy-start(s32[8,4,8]{2,1,0:T(4,128)} %param.10) | copy-start | bytes 3076
  22.3 11.8 %all-to-all-start.1 = ((bf16[2,4,8,8,512]{4,3,2,0,1:T(8,128)(2,1)}), bf16[2,4,8,8,512]{4,3,2,0,1:T(8,128)(2,1)S(1)}, u32[]{:S(2)}, u32[]{:S(2)}) async-start(bf16[2,4,8,8,512]{4,3,2,0,1:T(8,128)(2,1)} %copy_select_fusion.1), calls=%async_computation.1 | async-start | bytes 1048576 | tf_op jit(solution)/shard_map/all_to_all | solution.py:25
  35.7 1.0 %copy-start.2 = (f32[8,4,8,512]{3,2,1,0:T(8,128)S(1)}, f32[8,4,8,512]{3,2,1,0:T(8,128)}, u32[]{:S(2)}) copy-start(f32[8,4,8,512]{3,2,1,0:T(8,128)} %fusion.2) | copy-start | bytes 1572868
  36.8 43.0 %copy-start.6 = (f32[512]{0:T(512)S(1)}, f32[512]{0:T(512)}, u32[]{:S(2)}) copy-start(f32[512]{0:T(512)} %param.15) | copy-start | bytes 6148
  79.8 0.6 copy-start.4
where the time goes:
time: 83 us; the launch traced here: 82.5 us
  blocking collectives  41.5 us (50%)
  waiting for transfers between devices  16.3 us (20%)
  starting transfers between devices  9.83 us (12%)
  local copies, waits for them, and re-layouts  6.43 us (8%)
  matrix products  4.33 us (5%)
  other arithmetic  3.19 us (4%)
    psum x1, blocking collectives, per_device(): numerator, den = lax.psum((numerator, den), ('shot', 'rcv'))  41.5 us
    all_to_all x1, waiting for transfers between devices, per_device(): lax.all_to_all(stored, 'rcv', split_axis=2, concat_axis=1, tiled=True)  9.24 us
    all_to_all x1, waiting for transfers between devices, per_device(): lax.all_to_all(grouped, 'shot', split_axis=1, concat_axis=1, tiled=True)  7.09 us
    all_to_all x1, starting transfers between devices, per_device(): lax.all_to_all(stored, 'rcv', split_axis=2, concat_axis=1, tiled=True)  5.45 us
    all_to_all x1, starting transfers between devices, per_device(): lax.all_to_all(grouped, 'shot', split_axis=1, concat_axis=1, tiled=True)  4.38 us
    unnamed x19, local copies, waits for them, and re-layouts  4.35 us
    another operation x2, other arithmetic, per_device(): return (new_wavelet, jnp.stack([out_re, out_im]).astype(jnp.bfloat16))  2.1 us
    dot_general x2, matrix products, weigh(): jnp.dot(trace[1], coupling[0], preferred_element_type=jnp.float32)  1.73 us
  transfers between devices with their start and end apart: 2, of which 2 were waited for; matrix products, arithmetic and copies ran while one was open for 3% of the time, Pallas kernels for 0%

commit v1 on v0

--- a/solution.py
+++ b/solution.py
@@ -22,7 +22,10 @@
     spread = lax.all_to_all(stored, "rcv", split_axis=2, concat_axis=1, tiled=True)
     grouped = jnp.take(spread, shot_order, axis=1)
     grouped = grouped.reshape(2, slot_count, group_size, grouped.shape[2], grouped.shape[3])
-    arrived = lax.all_to_all(grouped, "shot", split_axis=1, concat_axis=1, tiled=True)
+    arrived = jnp.concatenate(
+        lax.all_to_all(jnp.stack(jnp.split(grouped, lax.axis_size("shot"), axis=1)), "shot", 0, 0),
+        axis=1,
+    )
     inverse = (
         jnp.zeros((line_count,), jnp.int32)
         .at[line_of_slot]

time: 83 us -> 83.1 us (level)
    another operation x0 -> x1, other arithmetic: none -> 0.86 us  [per_device(): jnp.stack(jnp.split(grouped, lax.axis_size('shot'), axis=1))]
where the time goes in v1:
time: 83.1 us; the launch traced here: 82.6 us
  blocking collectives  41.5 us (50%)
  waiting for transfers between devices  16.3 us (20%)
  starting transfers between devices  9.83 us (12%)
  local copies, waits for them, and re-layouts  6.46 us (8%)
  matrix products  4.32 us (5%)
  other arithmetic  3.26 us (4%)
    psum x1, blocking collectives, per_device(): numerator, den = lax.psum((numerator, den), ('shot', 'rcv'))  41.5 us
    all_to_all x1, waiting for transfers between devices, per_device(): lax.all_to_all(stored, 'rcv', split_axis=2, concat_axis=1, tiled=True)  9.26 us
    all_to_all x1, waiting for transfers between devices, per_device(): lax.all_to_all(jnp.stack(jnp.split(grouped, lax.axis_size('shot'), axis=1...  7.09 us
    all_to_all x1, starting transfers between devices, per_device(): lax.all_to_all(stored, 'rcv', split_axis=2, concat_axis=1, tiled=True)  5.45 us
    all_to_all x1, starting transfers between devices, per_device(): lax.all_to_all(jnp.stack(jnp.split(grouped, lax.axis_size('shot'), axis=1...  4.38 us
    unnamed x19, local copies, waits for them, and re-layouts  4.35 us
    another operation x2, other arithmetic, per_device(): return (new_wavelet, jnp.stack([out_re, out_im]).astype(jnp.bfloat16))  2.1 us
    dot_general x2, matrix products, weigh(): jnp.dot(trace[1], coupling[0], preferred_element_type=jnp.float32)  1.73 us
  transfers between devices with their start and end apart: 2, of which 2 were waited for; matrix products, arithmetic and copies ran while one was open for 3% of the time, Pallas kernels for 0%

profile of v1, /device:TPU:10, one launch (start us, length us, event | category | flops | bytes accessed | tf_op | source)
XLA Modules:
  0.0 82.6 jit_solution(17346934182558155640)
XLA Ops:
  0.6 0.0 copy-start
  0.6 2.3 %copy.41 = bf16[2,1,4,64,512]{4,2,0,3,1:T(4,128)(2,1)} copy(bf16[2,1,4,64,512]{4,3,2,1,0:T(8,128)(2,1)} %param.9) | data formatting | bytes 1048576 | tf_op args[1]
  3.0 5.5 %all-to-all-start = ((bf16[2,4,64,512]{3,1,0,2:T(4,128)(2,1)}), bf16[2,4,64,512]{3,1,0,2:T(4,128)(2,1)S(1)}, u32[]{:S(2)}, u32[]{:S(2)}) async-start(bf16[2,4,64,512]{3,1,0,2:T(4,128)(2,1)} %bitcast.84), calls=%async_computation | async-start | bytes 1048576 | tf_op jit(solution)/shard_map/all_to_all | solution.py:22
  8.4 0.0 copy-done.7
  8.4 0.0 copy-start.8
  8.5 0.6 copy-done.8
  9.1 0.1 broadcast_in_dim.31
  9.2 0.6 scatter_custom_fusion
  9.8 0.1 copy-done.3
  9.9 1.1 %fusion.2 = f32[8,4,8,512]{3,2,1,0:T(8,128)} fusion(bf16[2,512,512]{2,1,0:T(8,128)(2,1)S(1)} %copy-done, bf16[2,8,4,8,512]{4,3,2,1,0:T(8,128)(2,1)S(1)} %copy-done.1), kind=kOutput, calls=%fused_computation.11 | convolution fusion | flops 134217728 | bytes 1310720 | tf_op jit(solution)/shard_map/dot_general | solution.py:11
  11.0 0.3 fusion.10
  11.3 9.3 %all-to-all-done = bf16[2,4,64,512]{3,1,0,2:T(4,128)(2,1)S(1)} async-done(((bf16[2,4,64,512]{3,1,0,2:T(4,128)(2,1)}), bf16[2,4,64,512]{3,1,0,2:T(4,128)(2,1)S(1)}, u32[]{:S(2)}, u32[]{:S(2)}) %all-to-all-start) | async-done | bytes 524320 | tf_op jit(solution)/shard_map/all_to_all | solution.py:22
  20.5 0.2 copy.40
  20.7 0.6 gather_fusion
  21.3 0.1 copy_select_fusion.1
  21.5 0.9 %pad_maximum_fusion = bf16[4,2,1,8,8,512]{5,4,3,1,2,0:T(8,128)(2,1)} fusion(bf16[1,2,1,8,8,512]{5,4,3,1,2,0:T(8,128)(2,1)S(1)} %get-tuple-element.10, bf16[1,2,1,8,8,512]{5,4,3,1,2,0:T(8,128)(2,1)S(1)} %get-tuple-element.11, bf16[1,2,1,8,8,512]{5,4,3,1,2,0:T(8,128)(2,1)S(1)} %get-tuple-element.12, bf16[1,2,1,8,8,512]{5,4,3,1,2,0:T(8,128)(2,1)S(1)} %get-tuple-element.9), kind=kLoop, calls=%fused_computation.7 | loop fusion | flops 786432 | bytes 1048576 | tf_op jit(solution)/shard_map/stack | solution.py:26
  22.4 4.4 %all-to-all-start.1 = ((bf16[4,2,1,8,8,512]{5,4,3,1,2,0:T(8,128)(2,1)}), bf16[4,2,1,8,8,512]{5,4,3,1,2,0:T(8,128)(2,1)S(1)}, u32[]{:S(2)}, u32[]{:S(2)}) async-start(bf16[4,2,1,8,8,512]{5,4,3,1,2,0:T(8,128)(2,1)} %pad_maximum_fusion), calls=%async_computation.1 | async-start | bytes 1048576 | tf_op jit(solution)/shard_map/all_to_all | solution.py:26
  26.8 0.3 convolution_subtract_fusion.1
  27.1 7.1 %all-to-all-done.1 = bf16[4,2,1,8,8,512]{5,4,3,1,2,0:T(8,128)(2,1)S(1)} async-done(((bf16[4,2,1,8,8,512]{5,4,3,1,2,0:T(8,128)(2,1)}), bf16[4,2,1,8,8,512]{5,4,3,1,2,0:T(8,128)(2,1)S(1)}, u32[]{:S(2)}, u32[]{:S(2)}) %all-to-all-start.1) | async-done | bytes 524320 | tf_op jit(solution)/shard_map/all_to_all | solution.py:26
  34.2 0.6 gather_fusion.1
  34.8 0.1 fusion.12
  34.9 0.3 fusion
  35.2 0.3 fusion.8
  35.5 0.3 convolution_add_fusion
  35.9 0.3 convolution_subtract_fusion
  36.2 0.7 copy-done.2
  36.9 1.4 %add_reduce_fusion = (f32[512]{0:T(512)S(1)}, f32[512]{0:T(512)S(1)}, f32[512]{0:T(512)S(1)}, f32[8,4,8,512]{3,2,1,0:T(8,128)}) fusion(f32[8,4,8,512]{3,2,1,0:T(8,128)S(1)} %convolution_add_fusion, f32[8,4,8,512]{3,2,1,0:T(8,128)S(1)} %convolution_subtract_fusion.1, f32[8,4,8,512]{3,2,1,0:T(8,128)S(1)} %convolution_subtract_fusion, f32[512]{0:T(512)S(1)} %bitcast.93, ...), kind=kOutput, calls=%fused_computation.31 | convolution fusion | flops 137361920 | bytes 3434496 | tf_op jit(solution)/shard_map/dot_general | solution.py:11
  38.3 41.5 %all-reduce = (f32[2,512]{1,0:T(2,128)S(1)}, f32[512]{0:T(512)S(1)}) all-reduce(f32[2,512]{1,0:T(2,128)S(1)} %pad_maximum_fusion.2, f32[512]{0:T(512)S(1)} %get-tuple-element.4), channel_id=1, replica_groups=mesh['shot'=4,'rcv'=8] {'shot','rcv'}, use_global_device_ids=true, to_apply=%region_3.4 | all-reduce | flops 1536 | bytes 12288 | tf_op jit(solution)/shard_map/psum | solution.py:44
  79.9 0.0 copy-start.4
  79.9 0.6 copy-done.4
  80.5 1.3 %fusion.21 = (bf16[1,8,4,8,512]{4,3,2,1,0:T(8,128)(2,1)S(1)}, bf16[1,8,4,8,512]{4,3,2,1,0:T(8,128)(2,1)S(1)}) fusion(f32[8,4,8,512]{3,2,1,0:T(8,128)S(1)} %convolution_subtract_fusion, f32[8,4,8,512]{3,2,1,0:T(8,128)} %get-tuple-element.17, f32[8,4,8,512]{3,2,1,0:T(8,128)S(1)} %convolution_subtract_fusion.1, f32[512]{0:T(512)S(1)} %bitcast.91, ...), kind=kLoop, calls=%fused_computation.42 | loop fusion | flops 1572864 | bytes 2626560 | tf_op jit(solution)/shard_map/stack | solution.py:48
  81.7 0.8 %pad_maximum_fusion.1 = bf16[2,8,4,8,512]{4,3,2,1,0:T(8,128)(2,1)} fusion(bf16[1,8,4,8,512]{4,3,2,1,0:T(8,128)(2,1)S(1)} %get-tuple-element.8, bf16[1,8,4,8,512]{4,3,2,1,0:T(8,128)(2,1)S(1)} %get-tuple-element.7), kind=kLoop, calls=%fused_computation.8 | loop fusion | flops 262144 | bytes 1048576 | tf_op jit(solution)/shard_map/stack | solution.py:48
  (27 shorter events, 0.2 us)
Async XLA Ops:
  0.6 9.3 %copy-start = (bf16[2,512,512]{2,1,0:T(8,128)(2,1)S(1)}, bf16[2,512,512]{2,1,0:T(8,128)(2,1)}, u32[]{:S(2)}) copy-start(bf16[2,512,512]{2,1,0:T(8,128)(2,1)} %param.13) | copy-start | bytes 3145732
  3.0 5.5 %copy-start.7 = (s32[32]{0:T(128)S(1)}, s32[32]{0:T(128)}, u32[]{:S(2)}) copy-start(s32[32]{0:T(128)} %param.11) | copy-start | bytes 388
  3.0 6.9 %copy-start.1 = (bf16[2,8,4,8,512]{4,3,2,1,0:T(8,128)(2,1)S(1)}, bf16[2,8,4,8,512]{4,3,2,1,0:T(8,128)(2,1)}, u32[]{:S(2)}) copy-start(bf16[2,8,4,8,512]{4,3,2,1,0:T(8,128)(2,1)} %param.8) | copy-start | bytes 1572868
  3.0 17.6 %all-to-all-start = ((bf16[2,4,64,512]{3,1,0,2:T(4,128)(2,1)}), bf16[2,4,64,512]{3,1,0,2:T(4,128)(2,1)S(1)}, u32[]{:S(2)}, u32[]{:S(2)}) async-start(bf16[2,4,64,512]{3,1,0,2:T(4,128)(2,1)} %bitcast.84), calls=%async_computation | async-start | bytes 1048576 | tf_op jit(solution)/shard_map/all_to_all | solution.py:22
  8.4 0.7 copy-start.8
  9.2 0.7 copy-start.3
  22.4 4.4 %copy-start.5 = (s32[8,4,8]{2,1,0:T(4,128)S(1)}, s32[8,4,8]{2,1,0:T(4,128)}, u32[]{:S(2)}) copy-start(s32[8,4,8]{2,1,0:T(4,128)} %param.10) | copy-start | bytes 3076
  22.4 11.8 %all-to-all-start.1 = ((bf16[4,2,1,8,8,512]{5,4,3,1,2,0:T(8,128)(2,1)}), bf16[4,2,1,8,8,512]{5,4,3,1,2,0:T(8,128)(2,1)S(1)}, u32[]{:S(2)}, u32[]{:S(2)}) async-start(bf16[4,2,1,8,8,512]{5,4,3,1,2,0:T(8,128)(2,1)} %pad_maximum_fusion), calls=%async_computation.1 | async-start | bytes 1048576 | tf_op jit(solution)/shard_map/all_to_all | solution.py:26
  35.8 1.0 %copy-start.2 = (f32[8,4,8,512]{3,2,1,0:T(8,128)S(1)}, f32[8,4,8,512]{3,2,1,0:T(8,128)}, u32[]{:S(2)}) copy-start(f32[8,4,8,512]{3,2,1,0:T(8,128)} %fusion.2) | copy-start | bytes 1572868
  36.9 43.0 %copy-start.6 = (f32[512]{0:T(512)S(1)}, f32[512]{0:T(512)}, u32[]{:S(2)}) copy-start(f32[512]{0:T(512)} %param.15) | copy-start | bytes 6148
  79.9 0.6 copy-start.4
